TPU v7x, 32 devices: a whole 2x2x4 slice. The times are simulated.
32 devices in a mesh: row: 4 (over z), col: 8 (over y, x, core).
Axes of the slice: x: 2, y: 2, z: 4, core: 2. Of those that a mesh axis runs over, the one named last changes fastest.
Arguments:
- weight: float32 [16384, 16384], P('row', 'col'), may hold values from -0.046875 to 0.046875
- leak: float32 [16384], P('col'), may hold values from 0.1 to 1
- rates: float32 [3, 256, 16384], P(None, 'row', 'col'), may hold values from -0.95 to 0.95
- cotangent: float32 [256, 16384], P('row', 'col'), may hold values from -2 to 2
Outputs:
- grad_input: float32 [256, 16384], P('row', 'col')
- grad_weight: float32 [16384, 16384], P('row', 'col')
- grad_noise: float32 [3, 16384], P(None, 'row')
All inputs are finite; a program needn't handle non-finite values.
Results may differ from a plain program's by a relative error of at most 0.0001.
Values sent between devices are 32-bit elements; how exact they have to be, the bound alone decides.
A program may use at most 192 MiB of HBM per device.

v0:
```python
import jax
import jax.numpy as jnp
from jax import lax
from jax.sharding import PartitionSpec as P

TSTEPS = 3


def shards(weight, leak, rates, cotangent):
    n_col = lax.axis_size("col")
    own_rows = cotangent.shape[0]
    local_units = cotangent.shape[1]
    full_rates = lax.all_gather(rates, "row", axis=1, tiled=True)
    grad_weight = jnp.zeros(weight.shape, jnp.float32)
    noise_list = []
    carried = cotangent
    for step_back in range(TSTEPS - 1, -1, -1):
        scaled = leak[None, :] * carried
        spread = scaled.reshape(own_rows, local_units // n_col, n_col)
        by_col = lax.all_to_all(spread, "col", split_axis=2, concat_axis=1, tiled=True)
        by_row = lax.all_to_all(by_col, "row", split_axis=1, concat_axis=0, tiled=True)
        gathered = lax.all_gather(by_row, "col", axis=2, tiled=True)
        unit_block = gathered.reshape(gathered.shape[0], gathered.shape[1] * gathered.shape[2])
        rates_now = full_rates[step_back]
        noise_list.insert(0, jnp.sum(unit_block, axis=0))
        grad_weight = grad_weight + lax.dot_general(
            unit_block,
            rates_now,
            (((0,), (0,)), ((), ())),
            precision=lax.Precision.HIGHEST,
            preferred_element_type=jnp.float32,
        )
        partial_sum = jnp.dot(
            unit_block, weight, precision=lax.Precision.HIGHEST, preferred_element_type=jnp.float32
        )
        adjoint = lax.psum_scatter(partial_sum, "row", scatter_dimension=0, tiled=True)
        local_rates = rates[step_back]
        carried = (1.0 - leak[None, :]) * carried + (1.0 - local_rates * local_rates) * adjoint
    return (carried, grad_weight, jnp.stack(noise_list))


def solution(mesh):
    placed = (P("row", "col"), P("col"), P(None, "row", "col"), P("row", "col"))
    return jax.shard_map(
        shards,
        mesh=mesh,
        in_specs=placed,
        out_specs=(P("row", "col"), P("row", "col"), P(None, "row")),
        check_vma=False,
    )
```

profile of v0, /device:TPU:0, one launch (start us, length us, event | category | flops | bytes accessed | tf_op | source)
XLA Modules:
  0.0 634.5 jit_solution(5892808969612367369)
XLA Ops:
  9.0 14.7 %all_to_all.108 = f32[64,256,8]{1,0,2:T(8,128)S(1)} all-to-all(f32[64,256,8]{1,0,2:T(8,128)S(1)} %copy.20), channel_id=1, replica_groups=mesh['row'=4,'col'=8] {'col'}, dimensions={2} | all-to-all | bytes 1048576 | tf_op jit(solution)/shard_map/all_to_all | solution.py:20
  24.6 9.3 %reduce.3 = f32[2048,64]{1,0:T(8,128)S(1)} reduce(f32[2048,1,64]{2,1,0:T(1,128)S(1)} %bitcast.75, f32[]{:T(128)} %broadcast.24), dimensions={1}, to_apply=%bitcast.64.reduce_sub_computation | reduce | bytes 1048580
  34.6 18.6 %all_to_all.109 = f32[4,1,32768]{2,1,0:T(1,128)S(1)} all-to-all(f32[4,1,32768]{2,1,0:T(1,128)S(1)} %reshape.48), channel_id=1, replica_groups=mesh['row'=4,'col'=8] {'row'}, dimensions={0} | all-to-all | bytes 1048576 | tf_op jit(solution)/shard_map/all_to_all | solution.py:21
  58.3 34.2 %all-gather.5.cloned.1.call-done = f32[256,512,8]{1,0,2:T(8,128)} async-done(((f32[256,512,1]{1,0,2:T(8,128)}), f32[256,512,8]{1,0,2:T(8,128)}) %all-gather.5.cloned.1.call-update) | async-done | bytes 4194320 | tf_op jit(solution)/shard_map/all_gather | solution.py:22
  92.6 5.4 copy.25
  98.0 33.9 %fusion.9 = f32[256,2048]{1,0:T(8,128)} fusion(f32[4096,2048]{1,0:T(8,128)} %param.4, f32[256,512,8]{0,2,1:T(8,128)} %copy.25), kind=kOutput, calls=%fused_computation.10 | convolution fusion | flops 25769803776 | bytes 39845888 | tf_op jit(solution)/shard_map/dot_general | solution.py:33
  132.0 43.7 %reduce-scatter.4.cloned.1.call-done = f32[64,2048]{1,0:T(8,128)} async-done(((f32[256,2048]{1,0:T(8,128)}), f32[64,2048]{1,0:T(8,128)}) %reduce-scatter.4.cloned.1.call-update) | async-done | bytes 524304 | tf_op jit(solution)/shard_map/reduce_scatter | solution.py:36
  177.7 13.7 %all_to_all.110 = f32[64,256,8]{1,0,2:T(8,128)S(1)} all-to-all(f32[64,256,8]{1,0,2:T(8,128)S(1)} %copy.27), channel_id=1, replica_groups=mesh['row'=4,'col'=8] {'col'}, dimensions={2} | all-to-all | bytes 1048576 | tf_op jit(solution)/shard_map/all_to_all | solution.py:20
  191.8 9.3 %reduce.5 = f32[2048,64]{1,0:T(8,128)S(1)} reduce(f32[2048,1,64]{2,1,0:T(1,128)S(1)} %bitcast.76, f32[]{:T(128)} %broadcast.24), dimensions={1}, to_apply=%bitcast.66.reduce_sub_computation | reduce | bytes 1048580
  201.8 16.6 %all_to_all.111 = f32[4,1,32768]{2,1,0:T(1,128)S(1)} all-to-all(f32[4,1,32768]{2,1,0:T(1,128)S(1)} %reshape.50), channel_id=1, replica_groups=mesh['row'=4,'col'=8] {'row'}, dimensions={0} | all-to-all | bytes 1048576 | tf_op jit(solution)/shard_map/all_to_all | solution.py:21
  223.4 34.3 %all-gather.7.cloned.1.call-done = f32[256,512,8]{1,0,2:T(8,128)} async-done(((f32[256,512,1]{1,0,2:T(8,128)}), f32[256,512,8]{1,0,2:T(8,128)}) %all-gather.7.cloned.1.call-update) | async-done | bytes 4194320 | tf_op jit(solution)/shard_map/all_gather | solution.py:22
  257.7 5.5 copy.32
  263.2 33.8 %fusion.5 = f32[256,2048]{1,0:T(8,128)} fusion(f32[4096,2048]{1,0:T(8,128)} %param.4, f32[256,512,8]{0,2,1:T(8,128)} %copy.32), kind=kOutput, calls=%fused_computation.6 | convolution fusion | flops 25769803776 | bytes 39845888 | tf_op jit(solution)/shard_map/dot_general | solution.py:33
  297.8 43.2 %reduce-scatter.6.cloned.1.call-done = f32[64,2048]{1,0:T(8,128)} async-done(((f32[256,2048]{1,0:T(8,128)}), f32[64,2048]{1,0:T(8,128)}) %reduce-scatter.6.cloned.1.call-update) | async-done | bytes 524304 | tf_op jit(solution)/shard_map/reduce_scatter | solution.py:36
  343.7 13.5 %all_to_all.112 = f32[64,256,8]{1,0,2:T(8,128)} all-to-all(f32[64,256,8]{1,0,2:T(8,128)S(1)} %copy.34), channel_id=1, replica_groups=mesh['row'=4,'col'=8] {'col'}, dimensions={2} | all-to-all | bytes 1048576 | tf_op jit(solution)/shard_map/all_to_all | solution.py:20
  358.5 10.3 %reduce.7 = f32[2048,64]{1,0:T(8,128)} reduce(f32[2048,1,64]{2,1,0:T(1,128)S(1)} %bitcast.77, f32[]{:T(128)} %broadcast.24), dimensions={1}, to_apply=%bitcast.68.reduce_sub_computation | reduce | bytes 1048580
  370.7 32.0 %all_to_all.113 = f32[4,1,32768]{2,1,0:T(1,128)S(1)} all-to-all(f32[4,1,32768]{2,1,0:T(1,128)S(1)} %reshape.52), channel_id=1, replica_groups=mesh['row'=4,'col'=8] {'row'}, dimensions={0} | all-to-all | bytes 1048576 | tf_op jit(solution)/shard_map/all_to_all | solution.py:21
  410.7 57.2 %all-gather.11.cloned.1.call-done = f32[3,256,2048]{2,1,0:T(8,128)} async-done(((f32[3,64,2048]{2,1,0:T(8,128)}), f32[3,256,2048]{2,1,0:T(8,128)}) %all-gather.11.cloned.1.call-update) | async-done | bytes 6291472 | tf_op jit(solution)/shard_map/all_gather | solution.py:13
  468.0 32.4 %fusion.7 = f32[4096,2048]{1,0:T(8,128)} fusion(f32[256,512,8]{0,2,1:T(8,128)} %copy.25, f32[3,256,2048]{2,1,0:T(8,128)} %all-gather.11.cloned.1.call-done), kind=kOutput, calls=%fused_computation.8 | convolution fusion | flops 25769803776 | bytes 39845888 | tf_op jit(solution)/shard_map/dot_general | solution.py:26
  500.4 2.7 reduce_sum.28
  503.4 32.7 %fusion.3 = f32[4096,2048]{1,0:T(8,128)} fusion(f32[256,512,8]{0,2,1:T(8,128)} %copy.32, f32[3,256,2048]{2,1,0:T(8,128)} %all-gather.11.cloned.1.call-done), kind=kOutput, calls=%fused_computation.4 | convolution fusion | flops 25769803776 | bytes 39845888 | tf_op jit(solution)/shard_map/dot_general | solution.py:26
  539.0 5.5 copy.39
  544.4 33.9 %fusion.1 = f32[256,2048]{1,0:T(8,128)} fusion(f32[4096,2048]{1,0:T(8,128)} %param.4, f32[256,512,8]{0,2,1:T(8,128)} %copy.39), kind=kOutput, calls=%fused_computation.2 | convolution fusion | flops 25769803776 | bytes 39845888 | tf_op jit(solution)/shard_map/dot_general | solution.py:33
  579.1 46.4 %add_add_fusion = f32[4096,2048]{1,0:T(8,128)} fusion(f32[4096,2048]{1,0:T(8,128)} %fusion.7, f32[4096,2048]{1,0:T(8,128)} %fusion.3, f32[256,512,8]{0,2,1:T(8,128)} %copy.39, f32[3,256,2048]{2,1,0:T(8,128)} %all-gather.11.cloned.1.call-done), kind=kOutput, calls=%fused_computation | convolution fusion | flops 25786580992 | bytes 106954752 | tf_op jit(solution)/shard_map/dot_general | solution.py:26
  (65 shorter events, 36.9 us)
Async XLA Ops:
  7.2 85.4 %all-gather.5.cloned.1.call-start = ((), (), s32[]{:S(2)}) async-start(), calls=%async_computation.9 | async-start | bytes 4718592 | tf_op jit(solution)/shard_map/all_gather | solution.py:22
  58.0 117.7 %reduce-scatter.4.cloned.1.call-start = ((), (), s32[]{:S(2)}) async-start(), calls=%async_computation.10 | async-start | bytes 2621440 | tf_op jit(solution)/shard_map/reduce_scatter | solution.py:36
  98.0 33.9 %copy-start.4 = (f32[2048]{0:T(1024)S(1)}, f32[2048]{0:T(1024)}, u32[]{:S(2)}) copy-start(f32[2048]{0:T(1024)} %param.5) | copy-start | bytes 24580
  98.0 77.7 %copy-start.1 = (f32[64,2048]{1,0:T(8,128)S(1)}, f32[64,2048]{1,0:T(8,128)}, u32[]{:S(2)}) copy-start(f32[64,2048]{1,0:T(8,128)} %param.7) | copy-start | bytes 1572868
  131.9 125.9 %all-gather.7.cloned.1.call-start = ((), (), s32[]{:S(2)}) async-start(), calls=%async_computation.11 | async-start | bytes 4718592 | tf_op jit(solution)/shard_map/all_gather | solution.py:22
  223.2 117.7 %reduce-scatter.6.cloned.1.call-start = ((), (), s32[]{:S(2)}) async-start(), calls=%async_computation.12 | async-start | bytes 2621440 | tf_op jit(solution)/shard_map/reduce_scatter | solution.py:36
  263.2 77.7 %copy-start.3 = (f32[64,2048]{1,0:T(8,128)S(1)}, f32[64,2048]{1,0:T(8,128)}, u32[]{:S(2)}) copy-start(f32[64,2048]{1,0:T(8,128)} %reduce-scatter.4.cloned.1.call-done) | copy-start | bytes 1572868
  297.1 43.8 %copy-start = (f32[3,64,2048]{2,1,0:T(8,128)S(1)}, f32[3,64,2048]{2,1,0:T(8,128)}, u32[]{:S(2)}) copy-start(f32[3,64,2048]{2,1,0:T(8,128)} %param.6) | copy-start | bytes 4718596
  297.1 170.9 %all-gather.11.cloned.1.call-start = ((), (), s32[]{:S(2)}) async-start(), calls=%async_computation.15 | async-start | bytes 7864320 | tf_op jit(solution)/shard_map/all_gather | solution.py:13
  297.7 238.3 %all-gather.9.cloned.1.call-start = ((), (), s32[]{:S(2)}) async-start(), calls=%async_computation.13 | async-start | bytes 4718592 | tf_op jit(solution)/shard_map/all_gather | solution.py:22
  407.5 217.9 %reduce-scatter.8.cloned.1.call-start = ((), (), s32[]{:S(2)}) async-start(), calls=%async_computation.14 | async-start | bytes 2621440 | tf_op jit(solution)/shard_map/reduce_scatter | solution.py:36
  579.1 46.4 %copy-start.2 = (f32[64,2048]{1,0:T(8,128)S(1)}, f32[64,2048]{1,0:T(8,128)}, u32[]{:S(2)}) copy-start(f32[64,2048]{1,0:T(8,128)} %get-tuple-element.4) | copy-start | bytes 1572868
Sparse Core Ops, SparseCore 0:
  58.1 34.4 all-gather.4
  132.0 43.6 reduce-scatter.3
  223.3 34.4 all-gather.6
  297.2 43.6 reduce-scatter.5
  342.3 125.6 all-gather.10
  469.7 34.7 all-gather.8
  578.5 41.7 reduce-scatter.7
where the time goes:
time: 642 us; the launch traced here: 634 us
  waiting for transfers between devices  213 us (33%)
  matrix products  213 us (33%)
  blocking collectives  109 us (17%)
  other arithmetic  50.4 us (8%)
  local copies, waits for them, and re-layouts  33 us (5%)
  between operations  14.6 us (2%)
    dot_general x3, matrix products, shards(): lax.dot_general(unit_block, rates_now, (((0,), (0,)), ((), ())), precisio...  111 us
    dot_general x3, matrix products, shards(): jnp.dot(unit_block, weight, precision=lax.Precision.HIGHEST, preferred_el...  102 us
    reduce_scatter x3, waiting for transfers between devices, shards(): lax.psum_scatter(partial_sum, 'row', scatter_dimension=0, tiled=True)  86.9 us
    all_gather x3, waiting for transfers between devices, shards(): gathered = lax.all_gather(by_row, 'col', axis=2, tiled=True)  68.6 us
    all_to_all x3, blocking collectives, shards(): lax.all_to_all(by_col, 'row', split_axis=1, concat_axis=0, tiled=True)  67.2 us
    all_gather x1, waiting for transfers between devices, shards(): full_rates = lax.all_gather(rates, 'row', axis=1, tiled=True)  57.2 us
    all_to_all x3, blocking collectives, shards(): lax.all_to_all(spread, 'col', split_axis=2, concat_axis=1, tiled=True)  41.9 us
    unnamed x3, other arithmetic  29 us
  transfers between devices with their start and end apart: 7, of which 5 were waited for; matrix products, arithmetic and copies ran while one was open for 22% of the time, Pallas kernels for 0%

commit v1 on v0

--- a/solution.py
+++ b/solution.py
@@ -1,9 +1,29 @@
+import functools
 import jax
 import jax.numpy as jnp
 from jax import lax
 from jax.sharding import PartitionSpec as P
 
 TSTEPS = 3
+
+
+def _set_pipes(piece_in, ax_name):
+    shaped = lax.axis_size(ax_name)
+    fresh, next_value = (shaped, lax.axis_index(ax_name))
+    value_now = piece_in.shape[1] // fresh
+    step_out = jnp.roll(piece_in, -next_value * value_now, 1)
+    in_order = [lax.slice_in_dim(step_out, 0, value_now, axis=1)]
+    hop_no = 1
+    while hop_no < fresh:
+        tmp = lax.slice_in_dim(step_out, hop_no * value_now, (hop_no + 1) * value_now, axis=1)
+        small = lax.ppermute(tmp, ax_name, [(c, (c + hop_no) % fresh) for c in range(fresh)])
+        in_order.append(small)
+        hop_no += 1
+    t_next = jnp.concatenate(in_order[::-1], 0)
+    return jnp.roll(t_next, (next_value + 1) * in_order[0].shape[0], 0)
+
+
+push_node = functools.partial(_set_pipes, ax_name="row")
 
 
 def shards(weight, leak, rates, cotangent):
@@ -18,7 +38,7 @@
         scaled = leak[None, :] * carried
         spread = scaled.reshape(own_rows, local_units // n_col, n_col)
         by_col = lax.all_to_all(spread, "col", split_axis=2, concat_axis=1, tiled=True)
-        by_row = lax.all_to_all(by_col, "row", split_axis=1, concat_axis=0, tiled=True)
+        by_row = push_node(by_col)
         gathered = lax.all_gather(by_row, "col", axis=2, tiled=True)
         unit_block = gathered.reshape(gathered.shape[0], gathered.shape[1] * gathered.shape[2])
         rates_now = full_rates[step_back]

time: 642 us -> 611 us (0.952)
  blocking collectives: 109 us -> 26.3 us
  waiting for transfers between devices: 213 us -> 287 us
  other arithmetic: 50.4 us -> 19.8 us
  starting transfers between devices: 1 us -> 20.7 us
  local copies, waits for them, and re-layouts: 33 us -> 20.5 us
    all_to_all x3 -> x0, blocking collectives: 67.2 us -> none  [shards(): lax.all_to_all(by_col, 'row', split_axis=1, concat_axis=0, tiled=True)]
    ppermute x0 -> x9, waiting for transfers between devices: none -> 29 us  [_set_pipes(): lax.ppermute(tmp, ax_name, [(c, (c + hop_no) % fresh) for c in range(fres...]
    unnamed x3 -> x0, other arithmetic: 29 us -> none
    all_gather x1, waiting for transfers between devices: 57.2 us -> 86 us  [shards(): full_rates = lax.all_gather(rates, 'row', axis=1, tiled=True)]
    all_to_all x3 -> x2, blocking collectives: 41.9 us -> 26.3 us  [shards(): lax.all_to_all(spread, 'col', split_axis=2, concat_axis=1, tiled=True)]
    ppermute x0 -> x9, starting transfers between devices: none -> 14.8 us  [_set_pipes(): lax.ppermute(tmp, ax_name, [(c, (c + hop_no) % fresh) for c in range(fres...]
    all_to_all x0 -> x1, waiting for transfers between devices: none -> 9.64 us  [shards(): lax.all_to_all(spread, 'col', split_axis=2, concat_axis=1, tiled=True)]
    unnamed x17 -> x10, local copies, waits for them, and re-layouts: 7.58 us -> 0.02 us
  transfers between devices with their start and end apart: 7 -> 17, of which waited for: 5 -> 12; matrix products, arithmetic and copies ran while one was open for 22% -> 20% of each run, Pallas kernels for 0% -> 0%
where the time goes in v1:
time: 611 us; the launch traced here: 602 us
  waiting for transfers between devices  287 us (47%)
  matrix products  213 us (35%)
  blocking collectives  26.3 us (4%)
  starting transfers between devices  20.7 us (3%)
  local copies, waits for them, and re-layouts  20.5 us (3%)
  other arithmetic  19.8 us (3%)
  between operations  14.5 us (2%)
    dot_general x3, matrix products, shards(): lax.dot_general(unit_block, rates_now, (((0,), (0,)), ((), ())), precisio...  111 us
    dot_general x3, matrix products, shards(): jnp.dot(unit_block, weight, precision=lax.Precision.HIGHEST, preferred_el...  102 us
    reduce_scatter x3, waiting for transfers between devices, shards(): lax.psum_scatter(partial_sum, 'row', scatter_dimension=0, tiled=True)  86.8 us
    all_gather x1, waiting for transfers between devices, shards(): full_rates = lax.all_gather(rates, 'row', axis=1, tiled=True)  86 us
    all_gather x3, waiting for transfers between devices, shards(): gathered = lax.all_gather(by_row, 'col', axis=2, tiled=True)  74.9 us
    ppermute x9, waiting for transfers between devices, _set_pipes(): lax.ppermute(tmp, ax_name, [(c, (c + hop_no) % fresh) for c in range(fres...  29 us
    all_to_all x2, blocking collectives, shards(): lax.all_to_all(spread, 'col', split_axis=2, concat_axis=1, tiled=True)  26.3 us
    all_gather x3, local copies, waits for them, and re-layouts, shards(): gathered = lax.all_gather(by_row, 'col', axis=2, tiled=True)  16.4 us
  transfers between devices with their start and end apart: 17, of which 12 were waited for; matrix products, arithmetic and copies ran while one was open for 20% of the time, Pallas kernels for 0%

profile of v1, /device:TPU:0, one launch (start us, length us, event | category | flops | bytes accessed | tf_op | source)
XLA Modules:
  0.0 602.0 jit_solution(12364587319581738368)
XLA Ops:
  9.8 5.2 all-to-all-start
  15.0 9.6 %all-to-all-done = f32[64,256,8]{1,0,2:T(8,128)S(1)} async-done(((f32[64,256,8]{1,0,2:T(8,128)}), f32[64,256,8]{1,0,2:T(8,128)S(1)}, u32[]{:S(2)}, u32[]{:S(2)}) %all-to-all-start) | async-done | bytes 524320 | tf_op jit(solution)/shard_map/all_to_all | solution.py:40
  32.7 3.6 collective-permute-done.1
  37.8 38.5 %all-gather.5.cloned.1.call-done = f32[256,512,8]{1,0,2:T(8,128)} async-done(((f32[256,512,1]{1,0,2:T(8,128)}), f32[256,512,8]{1,0,2:T(8,128)}) %all-gather.5.cloned.1.call-update) | async-done | bytes 4194320 | tf_op jit(solution)/shard_map/all_gather | solution.py:42
  76.4 5.5 copy.19
  81.9 33.9 %fusion.9 = f32[256,2048]{1,0:T(8,128)} fusion(f32[4096,2048]{1,0:T(8,128)} %param.8, f32[256,512,8]{0,2,1:T(8,128)} %copy.19), kind=kOutput, calls=%fused_computation.10 | convolution fusion | flops 25769803776 | bytes 39845888 | tf_op jit(solution)/shard_map/dot_general | solution.py:53
  115.8 43.7 %reduce-scatter.4.cloned.1.call-done = f32[64,2048]{1,0:T(8,128)} async-done(((f32[256,2048]{1,0:T(8,128)}), f32[64,2048]{1,0:T(8,128)}) %reduce-scatter.4.cloned.1.call-update) | async-done | bytes 524304 | tf_op jit(solution)/shard_map/reduce_scatter | solution.py:56
  161.6 13.2 %all_to_all.54 = f32[64,256,8]{1,0,2:T(8,128)S(1)} all-to-all(f32[64,256,8]{1,0,2:T(8,128)S(1)} %copy.21), channel_id=1, replica_groups=mesh['row'=4,'col'=8] {'col'}, dimensions={2} | all-to-all | bytes 1048576 | tf_op jit(solution)/shard_map/all_to_all | solution.py:40
  179.6 3.6 collective-permute-done.5
  183.2 4.0 collective-permute-done.4
  188.9 36.3 %all-gather.7.cloned.1.call-done = f32[256,512,8]{1,0,2:T(8,128)} async-done(((f32[256,512,1]{1,0,2:T(8,128)}), f32[256,512,8]{1,0,2:T(8,128)}) %all-gather.7.cloned.1.call-update) | async-done | bytes 4194320 | tf_op jit(solution)/shard_map/all_gather | solution.py:42
  225.3 5.5 copy.23
  230.7 33.8 %fusion.5 = f32[256,2048]{1,0:T(8,128)} fusion(f32[4096,2048]{1,0:T(8,128)} %param.8, f32[256,512,8]{0,2,1:T(8,128)} %copy.23), kind=kOutput, calls=%fused_computation.6 | convolution fusion | flops 25769803776 | bytes 39845888 | tf_op jit(solution)/shard_map/dot_general | solution.py:53
  265.3 43.2 %reduce-scatter.6.cloned.1.call-done = f32[64,2048]{1,0:T(8,128)} async-done(((f32[256,2048]{1,0:T(8,128)}), f32[64,2048]{1,0:T(8,128)}) %reduce-scatter.6.cloned.1.call-update) | async-done | bytes 524304 | tf_op jit(solution)/shard_map/reduce_scatter | solution.py:56
  311.2 13.1 %all_to_all.55 = f32[64,256,8]{1,0,2:T(8,128)S(1)} all-to-all(f32[64,256,8]{1,0,2:T(8,128)S(1)} %copy.25), channel_id=1, replica_groups=mesh['row'=4,'col'=8] {'col'}, dimensions={2} | all-to-all | bytes 1048576 | tf_op jit(solution)/shard_map/all_to_all | solution.py:40
  329.2 6.4 %collective-permute-done.8 = f32[64,512,1]{1,0,2:T(8,128)S(1)} collective-permute-done((f32[64,512,1]{1,0,2:T(8,128)S(1)}, f32[64,512,1]{1,0,2:T(8,128)S(1)}, u32[]{:S(2)}, u32[]{:S(2)}) %collective-permute-start.8) | collective-permute-done | bytes 131104 | tf_op jit(solution)/shard_map/ppermute | solution.py:19
  335.6 9.2 %collective-permute-done.7 = f32[64,512,1]{1,0,2:T(8,128)S(1)} collective-permute-done((f32[64,512,1]{1,0,2:T(8,128)S(1)}, f32[64,512,1]{1,0,2:T(8,128)S(1)}, u32[]{:S(2)}, u32[]{:S(2)}) %collective-permute-start.7) | collective-permute-done | bytes 131104 | tf_op jit(solution)/shard_map/ppermute | solution.py:19
  349.5 86.0 %all-gather.11.cloned.1.call-done = f32[3,256,2048]{2,1,0:T(8,128)} async-done(((f32[3,64,2048]{2,1,0:T(8,128)}), f32[3,256,2048]{2,1,0:T(8,128)}) %all-gather.11.cloned.1.call-update) | async-done | bytes 6291472 | tf_op jit(solution)/shard_map/all_gather | solution.py:33
  435.5 32.4 %fusion.7 = f32[4096,2048]{1,0:T(8,128)} fusion(f32[256,512,8]{0,2,1:T(8,128)} %copy.19, f32[3,256,2048]{2,1,0:T(8,128)} %all-gather.11.cloned.1.call-done), kind=kOutput, calls=%fused_computation.8 | convolution fusion | flops 25769803776 | bytes 39845888 | tf_op jit(solution)/shard_map/dot_general | solution.py:46
  467.9 2.7 reduce_sum.28
  470.9 32.5 %fusion.3 = f32[4096,2048]{1,0:T(8,128)} fusion(f32[256,512,8]{0,2,1:T(8,128)} %copy.23, f32[3,256,2048]{2,1,0:T(8,128)} %all-gather.11.cloned.1.call-done), kind=kOutput, calls=%fused_computation.4 | convolution fusion | flops 25769803776 | bytes 39845888 | tf_op jit(solution)/shard_map/dot_general | solution.py:46
  506.3 5.5 copy.27
  511.7 34.2 %fusion.1 = f32[256,2048]{1,0:T(8,128)} fusion(f32[4096,2048]{1,0:T(8,128)} %param.8, f32[256,512,8]{0,2,1:T(8,128)} %copy.27), kind=kOutput, calls=%fused_computation.2 | convolution fusion | flops 25769803776 | bytes 39845888 | tf_op jit(solution)/shard_map/dot_general | solution.py:53
  546.7 46.3 %add_add_fusion = f32[4096,2048]{1,0:T(8,128)} fusion(f32[4096,2048]{1,0:T(8,128)} %fusion.7, f32[4096,2048]{1,0:T(8,128)} %fusion.3, f32[256,512,8]{0,2,1:T(8,128)} %copy.27, f32[3,256,2048]{2,1,0:T(8,128)} %all-gather.11.cloned.1.call-done), kind=kOutput, calls=%fused_computation | convolution fusion | flops 25786580992 | bytes 106954752 | tf_op jit(solution)/shard_map/dot_general | solution.py:46
  (71 shorter events, 39.5 us)
Async XLA Ops:
  9.8 14.9 %all-to-all-start = ((f32[64,256,8]{1,0,2:T(8,128)}), f32[64,256,8]{1,0,2:T(8,128)S(1)}, u32[]{:S(2)}, u32[]{:S(2)}) async-start(f32[64,256,8]{1,0,2:T(8,128)} %copy.17), calls=%async_computation | async-start | bytes 1048576 | tf_op jit(solution)/shard_map/all_to_all | solution.py:40
  15.0 61.4 %all-gather.5.cloned.1.call-start = ((), (), s32[]{:S(2)}) async-start(), calls=%async_computation.6 | async-start | bytes 4718592 | tf_op jit(solution)/shard_map/all_gather | solution.py:42
  24.9 7.8 %collective-permute-start.2 = (f32[64,512,1]{1,0,2:T(8,128)S(1)}, f32[64,512,1]{1,0,2:T(8,128)S(1)}, u32[]{:S(2)}, u32[]{:S(2)}) collective-permute-start(f32[64,512,1]{1,0,2:T(8,128)S(1)} %get-tuple-element.16), channel_id=1, source_target_pairs={{0,8},{8,16},{16,24},{24,0},{1,9},{9,17},{17,25},{25,1},{2,10},{10... | collective-permute-start | bytes 393224 | tf_op jit(solution)/shard_map/ppermute | solution.py:19
  26.5 9.7 %collective-permute-start.1 = (f32[64,512,1]{1,0,2:T(8,128)S(1)}, f32[64,512,1]{1,0,2:T(8,128)S(1)}, u32[]{:S(2)}, u32[]{:S(2)}) collective-permute-start(f32[64,512,1]{1,0,2:T(8,128)S(1)} %get-tuple-element.17), channel_id=1, source_target_pairs={{0,16},{8,24},{16,0},{24,8},{1,17},{9,25},{17,1},{25,9},{2,18},{10... | collective-permute-start | bytes 393224 | tf_op jit(solution)/shard_map/ppermute | solution.py:19
  29.1 7.2 %collective-permute-start = (f32[64,512,1]{1,0,2:T(8,128)S(1)}, f32[64,512,1]{1,0,2:T(8,128)S(1)}, u32[]{:S(2)}, u32[]{:S(2)}) collective-permute-start(f32[64,512,1]{1,0,2:T(8,128)S(1)} %get-tuple-element.18), channel_id=1, source_target_pairs={{0,24},{8,0},{16,8},{24,16},{1,25},{9,1},{17,9},{25,17},{2,26},{10... | collective-permute-start | bytes 393224 | tf_op jit(solution)/shard_map/ppermute | solution.py:19
  37.8 121.7 %reduce-scatter.4.cloned.1.call-start = ((), (), s32[]{:S(2)}) async-start(), calls=%async_computation.7 | async-start | bytes 2621440 | tf_op jit(solution)/shard_map/reduce_scatter | solution.py:56
  81.9 33.9 %copy-start.4 = (f32[2048]{0:T(1024)S(1)}, f32[2048]{0:T(1024)}, u32[]{:S(2)}) copy-start(f32[2048]{0:T(1024)} %param.9) | copy-start | bytes 24580
  81.9 77.6 %copy-start.1 = (f32[64,2048]{1,0:T(8,128)S(1)}, f32[64,2048]{1,0:T(8,128)}, u32[]{:S(2)}) copy-start(f32[64,2048]{1,0:T(8,128)} %param.11) | copy-start | bytes 1572868
  115.8 109.5 %all-gather.7.cloned.1.call-start = ((), (), s32[]{:S(2)}) async-start(), calls=%async_computation.8 | async-start | bytes 4718592 | tf_op jit(solution)/shard_map/all_gather | solution.py:42
  174.9 8.2 %collective-permute-start.5 = (f32[64,512,1]{1,0,2:T(8,128)S(1)}, f32[64,512,1]{1,0,2:T(8,128)S(1)}, u32[]{:S(2)}, u32[]{:S(2)}) collective-permute-start(f32[64,512,1]{1,0,2:T(8,128)S(1)} %get-tuple-element.12), channel_id=1, source_target_pairs={{0,8},{8,16},{16,24},{24,0},{1,9},{9,17},{17,25},{25,1},{2,10},{10... | collective-permute-start | bytes 393224 | tf_op jit(solution)/shard_map/ppermute | solution.py:19
  175.7 11.5 %collective-permute-start.4 = (f32[64,512,1]{1,0,2:T(8,128)S(1)}, f32[64,512,1]{1,0,2:T(8,128)S(1)}, u32[]{:S(2)}, u32[]{:S(2)}) collective-permute-start(f32[64,512,1]{1,0,2:T(8,128)S(1)} %get-tuple-element.13), channel_id=1, source_target_pairs={{0,16},{8,24},{16,0},{24,8},{1,17},{9,25},{17,1},{25,9},{2,18},{10... | collective-permute-start | bytes 393224 | tf_op jit(solution)/shard_map/ppermute | solution.py:19
  177.1 10.1 %collective-permute-start.3 = (f32[64,512,1]{1,0,2:T(8,128)S(1)}, f32[64,512,1]{1,0,2:T(8,128)S(1)}, u32[]{:S(2)}, u32[]{:S(2)}) collective-permute-start(f32[64,512,1]{1,0,2:T(8,128)S(1)} %get-tuple-element.14), channel_id=1, source_target_pairs={{0,24},{8,0},{16,8},{24,16},{1,25},{9,1},{17,9},{25,17},{2,26},{10... | collective-permute-start | bytes 393224 | tf_op jit(solution)/shard_map/ppermute | solution.py:19
  188.7 119.7 %reduce-scatter.6.cloned.1.call-start = ((), (), s32[]{:S(2)}) async-start(), calls=%async_computation.9 | async-start | bytes 2621440 | tf_op jit(solution)/shard_map/reduce_scatter | solution.py:56
  230.7 77.7 %copy-start.3 = (f32[64,2048]{1,0:T(8,128)S(1)}, f32[64,2048]{1,0:T(8,128)}, u32[]{:S(2)}) copy-start(f32[64,2048]{1,0:T(8,128)} %reduce-scatter.4.cloned.1.call-done) | copy-start | bytes 1572868
  264.6 43.8 %copy-start = (f32[3,64,2048]{2,1,0:T(8,128)S(1)}, f32[3,64,2048]{2,1,0:T(8,128)}, u32[]{:S(2)}) copy-start(f32[3,64,2048]{2,1,0:T(8,128)} %param.10) | copy-start | bytes 4718596
  264.6 170.9 %all-gather.11.cloned.1.call-start = ((), (), s32[]{:S(2)}) async-start(), calls=%async_computation.12 | async-start | bytes 7864320 | tf_op jit(solution)/shard_map/all_gather | solution.py:33
  265.2 238.1 %all-gather.9.cloned.1.call-start = ((), (), s32[]{:S(2)}) async-start(), calls=%async_computation.10 | async-start | bytes 4718592 | tf_op jit(solution)/shard_map/all_gather | solution.py:42
  324.5 11.0 %collective-permute-start.8 = (f32[64,512,1]{1,0,2:T(8,128)S(1)}, f32[64,512,1]{1,0,2:T(8,128)S(1)}, u32[]{:S(2)}, u32[]{:S(2)}) collective-permute-start(f32[64,512,1]{1,0,2:T(8,128)S(1)} %get-tuple-element.8), channel_id=1, source_target_pairs={{0,8},{8,16},{16,24},{24,0},{1,9},{9,17},{17,25},{25,1},{2,10},{10... | collective-permute-start | bytes 393224 | tf_op jit(solution)/shard_map/ppermute | solution.py:19
  325.3 19.5 %collective-permute-start.7 = (f32[64,512,1]{1,0,2:T(8,128)S(1)}, f32[64,512,1]{1,0,2:T(8,128)S(1)}, u32[]{:S(2)}, u32[]{:S(2)}) collective-permute-start(f32[64,512,1]{1,0,2:T(8,128)S(1)} %get-tuple-element.9), channel_id=1, source_target_pairs={{0,16},{8,24},{16,0},{24,8},{1,17},{9,25},{17,1},{25,9},{2,18},{10... | collective-permute-start | bytes 393224 | tf_op jit(solution)/shard_map/ppermute | solution.py:19
  326.7 18.0 %collective-permute-start.6 = (f32[64,512,1]{1,0,2:T(8,128)S(1)}, f32[64,512,1]{1,0,2:T(8,128)S(1)}, u32[]{:S(2)}, u32[]{:S(2)}) collective-permute-start(f32[64,512,1]{1,0,2:T(8,128)S(1)} %get-tuple-element.10), channel_id=1, source_target_pairs={{0,24},{8,0},{16,8},{24,16},{1,25},{9,1},{17,9},{25,17},{2,26},{10... | collective-permute-start | bytes 393224 | tf_op jit(solution)/shard_map/ppermute | solution.py:19
  346.3 246.7 %reduce-scatter.8.cloned.1.call-start = ((), (), s32[]{:S(2)}) async-start(), calls=%async_computation.11 | async-start | bytes 2621440 | tf_op jit(solution)/shard_map/reduce_scatter | solution.py:56
  546.7 46.3 %copy-start.2 = (f32[64,2048]{1,0:T(8,128)S(1)}, f32[64,2048]{1,0:T(8,128)}, u32[]{:S(2)}) copy-start(f32[64,2048]{1,0:T(8,128)} %get-tuple-element.6) | copy-start | bytes 1572868
Sparse Core Ops, SparseCore 0:
  37.9 38.3 all-gather.4
  115.9 43.5 reduce-scatter.3
  188.8 36.4 all-gather.6
  264.7 43.6 reduce-scatter.5
  309.8 125.6 all-gather.10
  437.2 34.7 all-gather.8
  546.1 41.7 reduce-scatter.7
